TPU v7x, 32 devices: a whole 2x2x4 slice. The times are simulated.
32 devices in a mesh: section: 2 (over y), dp: 4 (over x, core), mp: 4 (over z).
Axes of the slice: x: 2, y: 2, z: 4, core: 2. Of those that a mesh axis runs over, the one named last changes fastest.
Arguments:
- activations: bfloat16 [2, 256, 4096], P(None, 'dp'), may hold values from -6 to 6
- cotangent: bfloat16 [2, 256, 4096], P(None, 'dp'), may hold values from -6 to 6
- norm_gain: float32 [2, 4096], P('section'), may hold values from 0.1 to 1.9
- w_up: bfloat16 [2, 4096, 8192], P('section', 'dp', 'mp'), may hold values from -0.09375 to 0.09375
- w_down: bfloat16 [2, 4096, 8192], P('section', 'dp', 'mp'), may hold values from -0.0625 to 0.0625
- gram_left: float32 [2, 128, 512, 512], P('section', ('dp', 'mp')), as said below
- gram_right: float32 [2, 128, 512, 512], P('section', ('dp', 'mp')), as said below
- root_left: bfloat16 [2, 128, 512, 512], P('section', ('dp', 'mp'))
- root_right: bfloat16 [2, 128, 512, 512], P('section', ('dp', 'mp'))
- owner_slot: int32 [2, 16, 8], replicated, may hold values from 0 to 127, as said below
- eighth: int32 [2, 16, 8], replicated, may hold values from 0 to 7, as said below
- refresh_phase: int32 [1], replicated, may hold values from 0 to 999999
Outputs:
- new_gram_left: float32 [2, 128, 512, 512], P('section', ('dp', 'mp'))
- new_gram_right: float32 [2, 128, 512, 512], P('section', ('dp', 'mp'))
- new_root_left: bfloat16 [2, 128, 512, 512], P('section', ('dp', 'mp'))
- new_root_right: bfloat16 [2, 128, 512, 512], P('section', ('dp', 'mp'))
- update_blocks: bfloat16 [2, 128, 512, 512], P('section', ('dp', 'mp'))
Inputs may be any that keep to these rules, and one draw needn't show every extreme that they name: `owner_slot`: for each section, a permutation of the 128 slots; the block of flat index f = i * 8 + j goes to a slot t with (t // 8) % (4) == f // 32. `eighth`: in each section and each run of 32 consecutive flat block indices, every value is taken by exactly 4 blocks. `gram_left`: symmetric positive definite. `gram_right`: symmetric positive definite.
All inputs are finite; a program needn't handle non-finite values.
Results may differ from a plain program's by a relative error of at most 0.025.
Values may be sent and summed in bfloat16 or wider, within the bound.
A program may use at most 192 MiB of HBM per device.

v0:
```python
import math
import jax
import jax.numpy as jnp
from jax import lax
from jax.sharding import PartitionSpec as P

BLK = 512
ITERS = 2
norm_epsilon = 1e-05
decay_rate = 0.9
ridge_shift = 0.001
highest = lax.Precision.HIGHEST


def passed_along(block, axis, distance):
    devices = range(lax.axis_size(axis))
    route = [(i - distance, i) for i in devices if i - distance in devices]
    return lax.ppermute(block, axis, route)


def normalize_values(values, gain_row):
    inverse_rms = lax.rsqrt(jnp.mean(values * values, axis=-1, keepdims=True) + norm_epsilon)
    return values * inverse_rms * gain_row


def silu_slope(pre_act):
    sigmoid_values = jax.nn.sigmoid(pre_act)
    return sigmoid_values * (1.0 + pre_act * (1.0 - sigmoid_values))


def inverse_root(matrix):
    matrix_order = matrix.shape[-1]
    identity = jnp.eye(matrix_order, dtype=jnp.float32)
    shifted = matrix + ridge_shift * identity
    factor = 2.5 / jnp.sqrt(jnp.sum(shifted * shifted))
    iterate = jnp.power(factor, 0.25) * identity
    moment = factor * shifted
    for sweep_no in range(ITERS):
        step_mat = 1.25 * identity - 0.25 * moment
        square = jnp.dot(step_mat, step_mat, precision=highest)
        fourth = jnp.dot(square, square, precision=highest)
        moment = jnp.dot(fourth, moment, precision=highest)
        iterate = jnp.dot(iterate, step_mat, precision=highest)
    return iterate


def forward_layer(inputs, gain_row, up_rows, down_rows):
    values = inputs.astype(jnp.float32)
    normed = normalize_values(values, gain_row).astype(jnp.bfloat16)
    pre_act = jnp.dot(normed, up_rows, preferred_element_type=jnp.float32)
    hidden = jax.nn.silu(pre_act).astype(jnp.bfloat16)
    partial_value = lax.dot_general(
        hidden, down_rows, (((1,), (1,)), ((), ())), preferred_element_type=jnp.float32
    )
    branch = lax.psum(partial_value.astype(jnp.bfloat16), "mp").astype(jnp.float32)
    output = (values + branch).astype(jnp.bfloat16)
    return (output, pre_act, hidden)


def backward_layer(grad_output, inputs, pre_act, gain_row, up_rows, down_rows):
    grad_hidden = jnp.dot(grad_output, down_rows, preferred_element_type=jnp.float32)
    grad_pre = (grad_hidden * silu_slope(pre_act)).astype(jnp.bfloat16)
    partial_value = lax.dot_general(
        grad_pre, up_rows, (((1,), (1,)), ((), ())), preferred_element_type=jnp.float32
    )
    grad_normed = lax.psum(partial_value.astype(jnp.bfloat16), "mp").astype(jnp.float32)
    values = inputs.astype(jnp.float32)
    unused, pullback = jax.vjp(lambda values_in: normalize_values(values_in, gain_row), values)
    grad_values = pullback(grad_normed)[0]
    return (grad_output.astype(jnp.float32) + grad_values).astype(jnp.bfloat16)


def store_row(stack, entry, slot_index, is_valid):
    return jnp.where(is_valid, lax.dynamic_update_index_in_dim(stack, entry, slot_index, 0), stack)


def on_device(
    activations,
    cotangent,
    norm_gain,
    w_up,
    w_down,
    gram_left,
    gram_right,
    root_left,
    root_right,
    owner_slot,
    eighth,
    refresh_phase,
):
    section_no = lax.axis_index("section")
    dp_no = lax.axis_index("dp")
    mp_no = lax.axis_index("mp")
    section_total = lax.axis_size("section")
    dp_count = lax.axis_size("dp")
    mp_count = lax.axis_size("mp")
    micro_count, row_count, model_width = activations.shape
    gain_row = norm_gain[0]
    up_full, down_full = (
        lax.all_gather(w_up[0], "dp", axis=0, tiled=True),
        lax.all_gather(w_down[0], "dp", axis=0, tiled=True),
    )
    shard_ff = up_full.shape[1]
    tick_total = micro_count + section_total - 1
    inputs_all = jnp.zeros((micro_count, row_count, model_width), jnp.bfloat16)
    pre_all = jnp.zeros((micro_count, row_count, shard_ff), jnp.float32)
    hidden_all = jnp.zeros((micro_count, row_count, shard_ff), jnp.bfloat16)
    received = jnp.zeros((row_count, model_width), jnp.bfloat16)
    is_first = section_no == 0
    for tick_no in range(tick_total):
        batch_no = tick_no - section_no
        is_valid = (batch_no >= 0) & (batch_no < micro_count)
        slot_index = jnp.clip(batch_no, 0, micro_count - 1)
        inputs = jnp.where(is_first, activations[min(tick_no, micro_count - 1)], received)
        output, pre_act, hidden = forward_layer(inputs, gain_row, up_full, down_full)
        inputs_all = store_row(inputs_all, inputs, slot_index, is_valid)
        pre_all = store_row(pre_all, pre_act, slot_index, is_valid)
        hidden_all = store_row(hidden_all, hidden, slot_index, is_valid)
        if tick_no < tick_total - 1:
            received = passed_along(output, "section", 1)
    grad_all = jnp.zeros((micro_count, row_count, model_width), jnp.bfloat16)
    received = jnp.zeros((row_count, model_width), jnp.bfloat16)
    is_last = section_no == section_total - 1
    for tick_no in range(tick_total):
        batch_no = tick_no - (section_total - 1 - section_no)
        is_valid = (batch_no >= 0) & (batch_no < micro_count)
        slot_index = jnp.clip(batch_no, 0, micro_count - 1)
        grad_output = jnp.where(is_last, cotangent[min(tick_no, micro_count - 1)], received)
        inputs = lax.dynamic_index_in_dim(inputs_all, slot_index, 0, keepdims=False)
        pre_act = lax.dynamic_index_in_dim(pre_all, slot_index, 0, keepdims=False)
        grad_all = store_row(grad_all, grad_output, slot_index, is_valid)
        grad_input = backward_layer(grad_output, inputs, pre_act, gain_row, up_full, down_full)
        if tick_no < tick_total - 1:
            received = passed_along(grad_input, "section", -1)
    token_count = micro_count * row_count
    block_rows = shard_ff // BLK
    block_cols = model_width // BLK
    group_size = block_rows * block_cols
    per_dev = group_size // dp_count
    hidden_flat = hidden_all.reshape(token_count, block_rows, BLK)
    grad_flat = grad_all.reshape(token_count, block_cols, BLK)
    section_owner = lax.dynamic_index_in_dim(owner_slot, section_no, 0, keepdims=False)
    local_owner = lax.dynamic_slice_in_dim(
        section_owner, mp_no * block_rows, block_rows, 0
    ).reshape(-1)
    local_slot = local_owner // (mp_count * per_dev) * per_dev + local_owner % per_dev
    block_of_slot = jnp.argsort(local_slot)
    row_of_slot = block_of_slot // block_cols
    col_of_slot = block_of_slot % block_cols
    hidden_slots = jnp.take(hidden_flat, row_of_slot, axis=1)
    grad_slots = jnp.take(grad_flat, col_of_slot, axis=1)
    hidden_recv, grad_recv = (
        lax.all_to_all(hidden_slots, "dp", split_axis=1, concat_axis=0, tiled=True),
        lax.all_to_all(grad_slots, "dp", split_axis=1, concat_axis=0, tiled=True),
    )
    hidden_in = hidden_recv.reshape(dp_count, token_count, per_dev, BLK)
    grad_in = grad_recv.reshape(dp_count, token_count, per_dev, BLK)
    products = jnp.einsum("snbk,snbl->sbkl", hidden_in, grad_in, preferred_element_type=jnp.float32)
    rounded = lax.optimization_barrier(products.astype(jnp.bfloat16)).astype(jnp.float32)
    summed = jnp.sum(rounded, axis=0)
    scaled = summed * (1.0 / math.sqrt(token_count * dp_count))
    left_new = (
        decay_rate * gram_left[0]
        + jnp.einsum("sij,skj->sik", scaled, scaled, precision=highest) / BLK
    )
    right_new = (
        decay_rate * gram_right[0]
        + jnp.einsum("sji,sjk->sik", scaled, scaled, precision=highest) / BLK
    )
    phase_now = refresh_phase[0] % 8
    section_eighth = lax.dynamic_index_in_dim(eighth, section_no, 0, keepdims=False)
    local_eighth = lax.dynamic_slice_in_dim(
        section_eighth, mp_no * block_rows, block_rows, 0
    ).reshape(-1)
    is_due = jnp.take(local_eighth, block_of_slot) == phase_now
    my_due = lax.dynamic_slice_in_dim(is_due, dp_no * per_dev, per_dev)

    def refresh_slot(operands):
        return lax.cond(
            operands[0],
            lambda ops: (
                inverse_root(ops[1]).astype(jnp.bfloat16),
                inverse_root(ops[2]).astype(jnp.bfloat16),
            ),
            lambda ops: (ops[3], ops[4]),
            operands,
        )

    roots_l, roots_r = lax.map(
        refresh_slot, (my_due, left_new, right_new, root_left[0], root_right[0])
    )
    grad_low = scaled.astype(jnp.bfloat16)
    inner_product = jnp.einsum(
        "sij,sjk->sik", grad_low, roots_r, preferred_element_type=jnp.float32
    ).astype(jnp.bfloat16)
    update = jnp.einsum(
        "sij,sjk->sik", roots_l, inner_product, preferred_element_type=jnp.float32
    ).astype(jnp.bfloat16)
    return (left_new[None], right_new[None], roots_l[None], roots_r[None], update[None])


def solution(mesh):
    return jax.shard_map(
        on_device,
        mesh=mesh,
        in_specs=(
            P(None, "dp", None),
            P(None, "dp", None),
            P("section", None),
            P("section", "dp", "mp"),
            P("section", "dp", "mp"),
            P("section", ("dp", "mp"), None, None),
            P("section", ("dp", "mp"), None, None),
            P("section", ("dp", "mp"), None, None),
            P("section", ("dp", "mp"), None, None),
            P(),
            P(),
            P(),
        ),
        out_specs=(
            P("section", ("dp", "mp"), None, None),
            P("section", ("dp", "mp"), None, None),
            P("section", ("dp", "mp"), None, None),
            P("section", ("dp", "mp"), None, None),
            P("section", ("dp", "mp"), None, None),
        ),
        check_vma=False,
    )
```

profile of v0, /device:TPU:0, one launch (start us, length us, event | category | flops | bytes accessed | tf_op | source)
XLA Modules:
  0.0 786.2 jit_solution(6627781290026587765)
XLA Ops:
  9.0 109.2 %all-gather.5.cloned.1.call-done = bf16[1,4096,2048]{2,1,0:T(8,128)(2,1)} async-done(((bf16[1,1024,2048]{2,1,0:T(8,128)(2,1)}), bf16[1,4096,2048]{2,1,0:T(8,128)(2,1)}) %all-gather.5.cloned.1.call-update) | async-done | bytes 16777232 | tf_op jit(solution)/shard_map/all_gather | solution.py:100
  118.3 8.9 %bitcast_dynamic-update-slice_fusion.1 = (bf16[2,64,2048]{2,1,0:T(8,128)(2,1)S(1)}, f32[64,2048]{1,0:T(8,128)S(1)}) fusion(bf16[2,64,2048]{2,1,0:T(8,128)(2,1)S(1)} %broadcast_in_dim.113, s32[]{:T(128)S(6)} %min.19, pred[]{:T(512)S(6)} %and.63, bf16[1,4096,2048]{2,1,0:T(8,128)(2,1)} %all-gather.5.cloned.1.call-done, f32[4096]{0:T(1024)S(1)} %bitcast.238, ...), kind=kOutput, calls=%fused_computation.236 | convolution fusion | flops 1075838976 | bytes 18104838 | tf_op jit(solution)/shard_map/dot_general | solution.py:50
  127.2 98.5 %all-gather.7.cloned.1.call-done = bf16[1,4096,2048]{2,1,0:T(8,128)(2,1)} async-done(((bf16[1,1024,2048]{2,1,0:T(8,128)(2,1)}), bf16[1,4096,2048]{2,1,0:T(8,128)(2,1)}) %all-gather.7.cloned.1.call-update) | async-done | bytes 16777232 | tf_op jit(solution)/shard_map/all_gather | solution.py:101
  225.7 11.7 %fusion.108 = bf16[64,4096]{1,0:T(8,128)(2,1)} fusion(bf16[1,4096,2048]{2,1,0:T(8,128)(2,1)} %all-gather.7.cloned.1.call-done, f32[64,2048]{1,0:T(8,128)S(1)} %get-tuple-element.165), kind=kOutput, calls=%fused_computation.130 | convolution fusion | flops 1074659328 | bytes 17825792 | tf_op jit(solution)/shard_map/dot_general | solution.py:52
  237.5 38.7 %all-reduce.5.cloned.1.call-done = bf16[64,4096]{1,0:T(8,128)(2,1)} async-done(((bf16[64,4096]{1,0:T(8,128)(2,1)}), bf16[64,4096]{1,0:T(8,128)(2,1)}) %all-reduce.5.cloned.1.call-update) | async-done | bytes 524304 | tf_op jit(solution)/shard_map/psum | solution.py:55
  281.3 9.8 %collective-permute-done = bf16[64,4096]{1,0:T(8,128)(2,1)S(1)} collective-permute-done((bf16[64,4096]{1,0:T(8,128)(2,1)S(1)}, bf16[64,4096]{1,0:T(8,128)(2,1)S(1)}, u32[]{:S(2)}, u32[]{:S(2)}) %collective-permute-start) | collective-permute-done | bytes 524320 | tf_op jit(solution)/shard_map/ppermute | solution.py:18
  291.6 9.7 %fusion.198 = (bf16[2,64,2048]{2,1,0:T(8,128)(2,1)S(1)}, f32[64,2048]{1,0:T(8,128)}) fusion(bf16[2,64,2048]{2,1,0:T(8,128)(2,1)S(1)} %get-tuple-element.164, s32[]{:T(128)S(6)} %min.20, pred[]{:T(512)S(6)} %and.64, bf16[1,4096,2048]{2,1,0:T(8,128)(2,1)} %all-gather.5.cloned.1.call-done, bf16[64,4096]{1,0:T(8,128)(2,1)S(1)} %get-tuple-element.148, ...), kind=kOutput, calls=%fused_computation.235 | convolution fusion | flops 1075576832 | bytes 18366980 | tf_op jit(solution)/shard_map/dot_general | solution.py:50
  301.3 12.1 %fusion.111 = bf16[64,4096]{1,0:T(8,128)(2,1)} fusion(bf16[1,4096,2048]{2,1,0:T(8,128)(2,1)} %all-gather.7.cloned.1.call-done, f32[64,2048]{1,0:T(8,128)} %get-tuple-element.167), kind=kOutput, calls=%fused_computation.131 | convolution fusion | flops 1074659328 | bytes 17825792 | tf_op jit(solution)/shard_map/dot_general | solution.py:52
  316.2 36.6 %all-reduce.7.cloned.1.call-done = bf16[64,4096]{1,0:T(8,128)(2,1)} async-done(((bf16[64,4096]{1,0:T(8,128)(2,1)}), bf16[64,4096]{1,0:T(8,128)(2,1)}) %all-reduce.7.cloned.1.call-update) | async-done | bytes 524304 | tf_op jit(solution)/shard_map/psum | solution.py:55
  362.7 5.0 collective-permute-done.1
  368.1 9.0 %fusion.197 = (bf16[2,64,2048]{2,1,0:T(8,128)(2,1)S(1)}, f32[64,2048]{1,0:T(8,128)S(1)}) fusion(bf16[2,64,2048]{2,1,0:T(8,128)(2,1)S(1)} %copy-done.4, s32[]{:T(128)S(6)} %min.21, pred[]{:T(512)S(6)} %and.65, bf16[1,4096,2048]{2,1,0:T(8,128)(2,1)} %all-gather.5.cloned.1.call-done, bf16[64,4096]{1,0:T(8,128)(2,1)S(1)} %get-tuple-element.146, ...), kind=kOutput, calls=%fused_computation.233 | convolution fusion | flops 1075576832 | bytes 18366980 | tf_op jit(solution)/shard_map/dot_general | solution.py:50
  379.9 15.7 %fusion.102 = bf16[64,4096]{1,0:T(8,128)(2,1)} fusion(bf16[1,4096,2048]{2,1,0:T(8,128)(2,1)} %all-gather.5.cloned.1.call-done, bf16[1,4096,2048]{2,1,0:T(8,128)(2,1)} %all-gather.7.cloned.1.call-done, f32[2,64,2048]{2,1,0:T(8,128)} %fusion.180, s32[]{:T(128)S(6)} %min.22, bf16[2,64,4096]{2,1,0:T(8,128)(2,1)S(1)} %copy-done.2, pred[]{:T(512)S(6)} %eq.60), kind=kOutput, calls=%fused_computation.128 | convolution fusion | flops 2149187584 | bytes 35127300 | tf_op jit(solution)/shard_map/dot_general | solution.py:63
  397.6 37.3 %all-reduce.9.cloned.1.call-done = bf16[64,4096]{1,0:T(8,128)(2,1)} async-done(((bf16[64,4096]{1,0:T(8,128)(2,1)}), bf16[64,4096]{1,0:T(8,128)(2,1)}) %all-reduce.9.cloned.1.call-update) | async-done | bytes 524304 | tf_op jit(solution)/shard_map/psum | solution.py:66
  440.4 12.2 %collective-permute-done.2 = bf16[64,4096]{1,0:T(8,128)(2,1)} collective-permute-done((bf16[64,4096]{1,0:T(8,128)(2,1)S(1)}, bf16[64,4096]{1,0:T(8,128)(2,1)}, u32[]{:S(2)}, u32[]{:S(2)}) %collective-permute-start.2) | collective-permute-done | bytes 524320 | tf_op jit(solution)/shard_map/ppermute | solution.py:18
  454.9 15.8 %fusion.105 = bf16[64,4096]{1,0:T(8,128)(2,1)} fusion(bf16[1,4096,2048]{2,1,0:T(8,128)(2,1)} %all-gather.5.cloned.1.call-done, bf16[64,4096]{1,0:T(8,128)(2,1)S(1)} %get-tuple-element.144, bf16[1,4096,2048]{2,1,0:T(8,128)(2,1)} %all-gather.7.cloned.1.call-done, f32[2,64,2048]{2,1,0:T(8,128)} %fusion.180, s32[]{:T(128)S(6)} %min.23), kind=kOutput, calls=%fused_computation.129 | convolution fusion | flops 2148925440 | bytes 35127300 | tf_op jit(solution)/shard_map/dot_general | solution.py:63
  475.8 4.7 select_bitcast_fusion.1
  480.5 4.8 all-to-all-start
  485.4 22.8 %all-reduce.11.cloned.1.call-done = bf16[64,4096]{1,0:T(8,128)(2,1)} async-done(((bf16[64,4096]{1,0:T(8,128)(2,1)}), bf16[64,4096]{1,0:T(8,128)(2,1)}) %all-reduce.11.cloned.1.call-update) | async-done | bytes 524304 | tf_op jit(solution)/shard_map/psum | solution.py:66
  512.2 13.3 %collective-permute-done.3 = bf16[64,4096]{1,0:T(8,128)(2,1)S(1)} collective-permute-done((bf16[64,4096]{1,0:T(8,128)(2,1)S(1)}, bf16[64,4096]{1,0:T(8,128)(2,1)S(1)}, u32[]{:S(2)}, u32[]{:S(2)}) %collective-permute-start.3) | collective-permute-done | bytes 524320 | tf_op jit(solution)/shard_map/ppermute | solution.py:18
  532.3 4.7 select_bitcast_fusion
  537.0 5.0 all-to-all-start.1
  542.1 6.4 copy.34
  548.6 41.7 %all-to-all-done.1 = bf16[128,32,512]{2,0,1:T(8,128)(2,1)} async-done(((bf16[128,32,512]{2,0,1:T(8,128)(2,1)}), bf16[128,32,512]{2,0,1:T(8,128)(2,1)}, u32[]{:S(2)}, u32[]{:S(2)}) %all-to-all-start.1) | async-done | bytes 4194336 | tf_op jit(solution)/shard_map/all_to_all | solution.py:154
  590.2 10.9 %convolution_convert_fusion.2 = bf16[4,8,512,512]{3,2,1,0:T(8,128)(2,1)} fusion(bf16[4,128,8,512]{1,3,2,0:T(8,128)(2,1)} %bitcast.236, bf16[4,128,8,512]{3,1,2,0:T(8,128)(2,1)} %bitcast.37), kind=kOutput, calls=%fused_computation.120 | convolution fusion | flops 2155872256 | bytes 25165824 | tf_op jit(solution)/shard_map/snbk,snbl->sbkl/dot_general | solution.py:158
  601.1 9.6 %convert_reduce_fusion = f32[8,512,512]{2,1,0:T(8,128)S(1)} fusion(bf16[4,8,512,512]{3,2,1,0:T(8,128)(2,1)} %convolution_convert_fusion.2), kind=kLoop, calls=%fused_computation.101 | loop fusion | flops 14680064 | bytes 25165824 | tf_op jit(solution)/shard_map/reduce_sum | solution.py:160
  610.7 19.7 %bitcast_add_fusion = f32[8,512,512]{2,1,0:T(8,128)} fusion(f32[1,8,512,512]{3,2,1,0:T(8,128)} %param.22, f32[8,512,512]{2,1,0:T(8,128)S(1)} %convert_reduce_fusion), kind=kOutput, calls=%fused_computation.121 | convolution fusion | flops 12893290496 | bytes 25165824 | tf_op jit(solution)/shard_map/sji,sjk->sik/dot_general | solution.py:168
  630.4 17.6 %bitcast_add_fusion.1 = f32[8,512,512]{2,1,0:T(8,128)} fusion(f32[1,8,512,512]{3,2,1,0:T(8,128)} %param.21, f32[8,512,512]{2,1,0:T(8,128)S(1)} %convert_reduce_fusion), kind=kOutput, calls=%fused_computation.122 | convolution fusion | flops 12893290496 | bytes 25165824 | tf_op jit(solution)/shard_map/sij,skj->sik/dot_general | solution.py:164
  648.0 118.6 %while.12 = (s32[]{:T(128)}, bf16[8,512,512]{2,1,0:T(8,128)(2,1)}, bf16[8,512,512]{2,1,0:T(8,128)(2,1)}, pred[8]{0:T(512)(128)(4,1)S(1)}, bf16[8,512,512]{2,1,0:...) while((s32[]{:T(128)}, bf16[8,512,512]{2,1,0:T(8,128)(2,1)}, ...), condition=%wide.region_18.19_spmd, body=%wide.region_13.18_spmd.sunk | while | flops 16121331712 | bytes 28315412 | solution.py:189
  660.1 31.2 %conditional.2 = (bf16[1,512,512]{2,1,0:T(8,128)(2,1)S(1)}, bf16[1,512,512]{2,1,0:T(8,128)(2,1)S(1)}) conditional(s32[]{:T(128)} %bitcast.230, (bf16[8,512,512]{2,1,0:T(8,128)(2,1)}, s32[]{:T(128)}, bf16[8,512,512]{2,1,0:T(8,128)(2,1)}) %tuple.65, (f32[8,512,512]{2,1,0:T(8,128)}, s32[]{:T(128)}, f32[8,512,512]{2,1,0:T(8,128)}) %tuple.66), branch_computations={%region_14.14_spmd, %region_15.17_spmd} | conditional | flops 16121331712 | bytes 26217596 | solution.py:179
  693.6 31.1 %conditional.2 = (bf16[1,512,512]{2,1,0:T(8,128)(2,1)S(1)}, bf16[1,512,512]{2,1,0:T(8,128)(2,1)S(1)}) conditional(s32[]{:T(128)} %bitcast.230, (bf16[8,512,512]{2,1,0:T(8,128)(2,1)}, s32[]{:T(128)}, bf16[8,512,512]{2,1,0:T(8,128)(2,1)}) %tuple.65, (f32[8,512,512]{2,1,0:T(8,128)}, s32[]{:T(128)}, f32[8,512,512]{2,1,0:T(8,128)}) %tuple.66), branch_computations={%region_14.14_spmd, %region_15.17_spmd} | conditional | flops 16121331712 | bytes 26217596 | solution.py:179
  727.1 31.1 %conditional.2 = (bf16[1,512,512]{2,1,0:T(8,128)(2,1)S(1)}, bf16[1,512,512]{2,1,0:T(8,128)(2,1)S(1)}) conditional(s32[]{:T(128)} %bitcast.230, (bf16[8,512,512]{2,1,0:T(8,128)(2,1)}, s32[]{:T(128)}, bf16[8,512,512]{2,1,0:T(8,128)(2,1)}) %tuple.65, (f32[8,512,512]{2,1,0:T(8,128)}, s32[]{:T(128)}, f32[8,512,512]{2,1,0:T(8,128)}) %tuple.66), branch_computations={%region_14.14_spmd, %region_15.17_spmd} | conditional | flops 16121331712 | bytes 26217596 | solution.py:179
  766.6 12.3 %convert_bitcast_fusion = bf16[1,8,512,512]{3,2,1,0:T(8,128)(2,1)} fusion(bf16[8,512,512]{2,1,0:T(8,128)(2,1)} %get-tuple-element.120, bf16[8,512,512]{2,1,0:T(8,128)(2,1)} %get-tuple-element.121, f32[8,512,512]{2,1,0:T(8,128)} %copy-done), kind=kOutput, calls=%fused_computation.135 | convolution fusion | flops 4303355904 | bytes 20971520 | tf_op jit(solution)/shard_map/sij,sjk->sik/dot_general | solution.py:196
  (148 shorter events, 162.9 us)
Async XLA Ops:
  7.2 1.6 copy-start.1
  7.2 111.1 %copy-start.8 = (f32[1,4096]{1,0:T(1,128)S(1)}, f32[1,4096]{1,0:T(1,128)}, u32[]{:S(2)}) copy-start(f32[1,4096]{1,0:T(1,128)} %param.18) | copy-start | bytes 49156
  7.2 111.0 %all-gather.5.cloned.1.call-start = ((), (), s32[]{:S(2)}) async-start(), calls=%async_computation.6 | async-start | bytes 20971520 | tf_op jit(solution)/shard_map/all_gather | solution.py:100
  7.9 217.8 %all-gather.7.cloned.1.call-start = ((), (), s32[]{:S(2)}) async-start(), calls=%async_computation.7 | async-start | bytes 20971520 | tf_op jit(solution)/shard_map/all_gather | solution.py:101
  8.7 267.6 %all-reduce.5.cloned.1.call-start = ((), (), s32[]{:S(2)}) async-start(), calls=%async_computation.2 | async-start | bytes 1048576 | tf_op jit(solution)/shard_map/psum | solution.py:55
  127.2 110.2 %copy-start.7 = (f32[64,2048]{1,0:T(8,128)}, f32[64,2048]{1,0:T(8,128)S(1)}, u32[]{:S(2)}) copy-start(f32[64,2048]{1,0:T(8,128)S(1)} %get-tuple-element.165) | copy-start | bytes 1572868
  237.5 115.3 %all-reduce.7.cloned.1.call-start = ((), (), s32[]{:S(2)}) async-start(), calls=%async_computation.3 | async-start | bytes 1048576 | tf_op jit(solution)/shard_map/psum | solution.py:55
  277.4 13.6 %collective-permute-start = (bf16[64,4096]{1,0:T(8,128)(2,1)S(1)}, bf16[64,4096]{1,0:T(8,128)(2,1)S(1)}, u32[]{:S(2)}, u32[]{:S(2)}) collective-permute-start(bf16[64,4096]{1,0:T(8,128)(2,1)S(1)} %fusion.152), channel_id=1, source_target_pairs={{0,16},{1,17},{2,18},{3,19},{4,20},{5,21},{6,22},{7,23},{8,24},{9,... | collective-permute-start | bytes 1572872 | tf_op jit(solution)/shard_map/ppermute | solution.py:18
  301.3 13.2 %copy-start.3 = (bf16[2,64,2048]{2,1,0:T(8,128)(2,1)}, bf16[2,64,2048]{2,1,0:T(8,128)(2,1)S(1)}, u32[]{:S(2)}) copy-start(bf16[2,64,2048]{2,1,0:T(8,128)(2,1)S(1)} %get-tuple-element.166) | copy-start | bytes 1572868
  301.3 12.9 %copy-start.9 = (s32[2,16,8]{1,2,0:T(8,128)S(1)}, s32[2,16,8]{1,2,0:T(8,128)}, u32[]{:S(2)}) copy-start(s32[2,16,8]{1,2,0:T(8,128)} %param.26) | copy-start | bytes 3076
  301.3 12.9 %copy-start.10 = (s32[2,16,8]{1,2,0:T(8,128)S(1)}, s32[2,16,8]{1,2,0:T(8,128)}, u32[]{:S(2)}) copy-start(s32[2,16,8]{1,2,0:T(8,128)} %param.25) | copy-start | bytes 3076
  313.4 121.6 %all-reduce.9.cloned.1.call-start = ((), (), s32[]{:S(2)}) async-start(), calls=%async_computation.4 | async-start | bytes 1048576 | tf_op jit(solution)/shard_map/psum | solution.py:66
  352.8 15.3 %copy-start.4 = (bf16[2,64,2048]{2,1,0:T(8,128)(2,1)S(1)}, bf16[2,64,2048]{2,1,0:T(8,128)(2,1)}, u32[]{:S(2)}) copy-start(bf16[2,64,2048]{2,1,0:T(8,128)(2,1)} %copy-done.3) | copy-start | bytes 1572868
  354.0 13.6 %collective-permute-start.1 = (bf16[64,4096]{1,0:T(8,128)(2,1)S(1)}, bf16[64,4096]{1,0:T(8,128)(2,1)S(1)}, u32[]{:S(2)}, u32[]{:S(2)}) collective-permute-start(bf16[64,4096]{1,0:T(8,128)(2,1)S(1)} %fusion.144), channel_id=1, source_target_pairs={{0,16},{1,17},{2,18},{3,19},{4,20},{5,21},{6,22},{7,23},{8,24},{9,... | collective-permute-start | bytes 1572872 | tf_op jit(solution)/shard_map/ppermute | solution.py:18
  368.1 11.7 %copy-start.2 = (bf16[2,64,4096]{2,1,0:T(8,128)(2,1)S(1)}, bf16[2,64,4096]{2,1,0:T(8,128)(2,1)}, u32[]{:S(2)}) copy-start(bf16[2,64,4096]{2,1,0:T(8,128)(2,1)} %param.17) | copy-start | bytes 3145732
  377.2 0.8 copy-start.5
  395.6 112.6 %all-reduce.11.cloned.1.call-start = ((), (), s32[]{:S(2)}) async-start(), calls=%async_computation.5 | async-start | bytes 1048576 | tf_op jit(solution)/shard_map/psum | solution.py:66
  437.9 14.7 %collective-permute-start.2 = (bf16[64,4096]{1,0:T(8,128)(2,1)S(1)}, bf16[64,4096]{1,0:T(8,128)(2,1)}, u32[]{:S(2)}, u32[]{:S(2)}) collective-permute-start(bf16[64,4096]{1,0:T(8,128)(2,1)S(1)} %fusion.146), channel_id=1, source_target_pairs={{16,0},{17,1},{18,2},{19,3},{20,4},{21,5},{22,6},{23,7},{24,8},{25... | collective-permute-start | bytes 1572872 | tf_op jit(solution)/shard_map/ppermute | solution.py:18
  454.9 15.8 %copy-start.6 = (bf16[2,64,2048]{2,1,0:T(8,128)(2,1)S(1)}, bf16[2,64,2048]{2,1,0:T(8,128)(2,1)}, u32[]{:S(2)}) copy-start(bf16[2,64,2048]{2,1,0:T(8,128)(2,1)} %copy-done.5) | copy-start | bytes 1572868
  480.5 56.5 %all-to-all-start = ((bf16[128,32,512]{2,0,1:T(8,128)(2,1)}), bf16[128,32,512]{2,0,1:T(8,128)(2,1)}, u32[]{:S(2)}, u32[]{:S(2)}) async-start(bf16[128,32,512]{2,0,1:T(8,128)(2,1)} %select_bitcast_fusion.1), calls=%async_computation | async-start | bytes 8388608 | tf_op jit(solution)/shard_map/all_to_all | solution.py:153
  510.9 14.6 %collective-permute-start.3 = (bf16[64,4096]{1,0:T(8,128)(2,1)S(1)}, bf16[64,4096]{1,0:T(8,128)(2,1)S(1)}, u32[]{:S(2)}, u32[]{:S(2)}) collective-permute-start(bf16[64,4096]{1,0:T(8,128)(2,1)S(1)} %fusion.148), channel_id=1, source_target_pairs={{16,0},{17,1},{18,2},{19,3},{20,4},{21,5},{22,6},{23,7},{24,8},{25... | collective-permute-start | bytes 1572872 | tf_op jit(solution)/shard_map/ppermute | solution.py:18
  537.0 53.2 %all-to-all-start.1 = ((bf16[128,32,512]{2,0,1:T(8,128)(2,1)}), bf16[128,32,512]{2,0,1:T(8,128)(2,1)}, u32[]{:S(2)}, u32[]{:S(2)}) async-start(bf16[128,32,512]{2,0,1:T(8,128)(2,1)} %select_bitcast_fusion), calls=%async_computation.1 | async-start | bytes 8388608 | tf_op jit(solution)/shard_map/all_to_all | solution.py:154
  610.7 19.7 %copy-start = (f32[8,512,512]{2,1,0:T(8,128)}, f32[8,512,512]{2,1,0:T(8,128)S(1)}, u32[]{:S(2)}) copy-start(f32[8,512,512]{2,1,0:T(8,128)S(1)} %convert_reduce_fusion) | copy-start | bytes 25165828
Sparse Core Ops, SparseCore 0:
  9.5 108.6 all-gather.4
  119.8 105.8 all-gather.6
  237.6 38.6 all-reduce.4
  313.5 39.2 all-reduce.6
  395.7 39.1 all-reduce.8
  470.8 37.3 all-reduce.10
where the time goes:
time: 794 us; the launch traced here: 786 us
  waiting for transfers between devices  427 us (54%)
  matrix products  225 us (28%)
  other arithmetic  48.4 us (6%)
  local copies, waits for them, and re-layouts  40 us (5%)
  starting transfers between devices  20.4 us (3%)
  between operations  15.6 us (2%)
  loops' own time  10.5 us (1%)
    all_gather x1, waiting for transfers between devices, on_device(): lax.all_gather(w_up[0], 'dp', axis=0, tiled=True)  109 us
    all_gather x1, waiting for transfers between devices, on_device(): lax.all_gather(w_down[0], 'dp', axis=0, tiled=True)  98.5 us
    psum x2, waiting for transfers between devices, forward_layer(): lax.psum(partial_value.astype(jnp.bfloat16), 'mp').astype(jnp.float32)  75.3 us
    psum x2, waiting for transfers between devices, backward_layer(): lax.psum(partial_value.astype(jnp.bfloat16), 'mp').astype(jnp.float32)  60.1 us
    all_to_all x1, waiting for transfers between devices, on_device(): lax.all_to_all(grad_slots, 'dp', split_axis=1, concat_axis=0, tiled=True)  41.7 us
    ppermute x4, waiting for transfers between devices, passed_along(): return lax.ppermute(block, axis, route)  40.3 us
    dot_general x2, matrix products, backward_layer(): lax.dot_general(grad_pre, up_rows, (((1,), (1,)), ((), ())), preferred_el...  31.5 us
    dot_general x12, matrix products, inverse_root(): iterate = jnp.dot(iterate, step_mat, precision=highest)  29.8 us
  transfers between devices with their start and end apart: 12, of which 11 were waited for; matrix products, arithmetic and copies ran while one was open for 6% of the time, Pallas kernels for 0%

commit v1 on v0

--- a/solution.py
+++ b/solution.py
@@ -10,6 +10,22 @@
 decay_rate = 0.9
 ridge_shift = 0.001
 highest = lax.Precision.HIGHEST
+
+
+def collect(x, axis, dim):
+    ways, here, step = (lax.axis_size(axis), lax.axis_index(axis), x.shape[dim])
+    dims = [n * ways if d == dim else n for d, n in enumerate(x.shape)]
+    full = lax.dynamic_update_slice_in_dim(jnp.zeros(dims, x.dtype), x, here * step, axis=dim)
+    going_up = going_down = x
+    for far in range(1, ways // 2 + 1):
+        going_up = lax.ppermute(going_up, axis, [(d, (d + 1) % ways) for d in range(ways)])
+        full = lax.dynamic_update_slice_in_dim(full, going_up, (here - far) % ways * step, axis=dim)
+        if 2 * far < ways:
+            going_down = lax.ppermute(going_down, axis, [(d, (d - 1) % ways) for d in range(ways)])
+            full = lax.dynamic_update_slice_in_dim(
+                full, going_down, (here + far) % ways * step, axis=dim
+            )
+    return full
 
 
 def passed_along(block, axis, distance):
@@ -98,7 +114,7 @@
     gain_row = norm_gain[0]
     up_full, down_full = (
         lax.all_gather(w_up[0], "dp", axis=0, tiled=True),
-        lax.all_gather(w_down[0], "dp", axis=0, tiled=True),
+        collect(w_down[0], "dp", 0),
     )
     shard_ff = up_full.shape[1]
     tick_total = micro_count + section_total - 1

time: 794 us -> 822 us (1.035)
  local copies, waits for them, and re-layouts: 40 us -> 63.2 us
  starting transfers between devices: 20.4 us -> 29.9 us
    ppermute x0 -> x3, waiting for transfers between devices: none -> 199 us  [the longest x2 199 us: collect(): lax.ppermute(going_up, axis, [(d, (d + 1) % ways) for d in range(ways)])]
    all_gather x1, waiting for transfers between devices: 109 us -> 0.01 us  [on_device(): lax.all_gather(w_up[0], 'dp', axis=0, tiled=True)]
    all_gather x1 -> x0, waiting for transfers between devices: 98.5 us -> none  [on_device(): lax.all_gather(w_down[0], 'dp', axis=0, tiled=True)]
    dynamic_update_slice x0 -> x4, local copies, waits for them, and re-layouts: none -> 16.5 us  [the longest x2 9.45 us: collect(): lax.dynamic_update_slice_in_dim(full, going_up, (here - far) % ways * ste...]
    ppermute x0 -> x3, starting transfers between devices: none -> 9.47 us  [the longest x2 7.49 us: collect(): lax.ppermute(going_up, axis, [(d, (d + 1) % ways) for d in range(ways)])]
  transfers between devices with their start and end apart: 12 -> 14, of which waited for: 11 -> 11; matrix products, arithmetic and copies ran while one was open for 6% -> 8% of each run, Pallas kernels for 0% -> 0%
where the time goes in v1:
time: 822 us; the launch traced here: 813 us
  waiting for transfers between devices  420 us (51%)
  matrix products  225 us (27%)
  local copies, waits for them, and re-layouts  63.2 us (8%)
  other arithmetic  49.5 us (6%)
  starting transfers between devices  29.9 us (4%)
  between operations  15.3 us (2%)
  loops' own time  10.6 us (1%)
    ppermute x2, waiting for transfers between devices, collect(): lax.ppermute(going_up, axis, [(d, (d + 1) % ways) for d in range(ways)])  199 us
    psum x2, waiting for transfers between devices, forward_layer(): lax.psum(partial_value.astype(jnp.bfloat16), 'mp').astype(jnp.float32)  77.2 us
    psum x2, waiting for transfers between devices, backward_layer(): lax.psum(partial_value.astype(jnp.bfloat16), 'mp').astype(jnp.float32)  60.1 us
    all_to_all x1, waiting for transfers between devices, on_device(): lax.all_to_all(grad_slots, 'dp', split_axis=1, concat_axis=0, tiled=True)  41.7 us
    ppermute x4, waiting for transfers between devices, passed_along(): return lax.ppermute(block, axis, route)  40.3 us
    dot_general x2, matrix products, backward_layer(): lax.dot_general(grad_pre, up_rows, (((1,), (1,)), ((), ())), preferred_el...  31.5 us
    dot_general x12, matrix products, inverse_root(): iterate = jnp.dot(iterate, step_mat, precision=highest)  29.8 us
    dot_general x3, matrix products, forward_layer(): pre_act = jnp.dot(normed, up_rows, preferred_element_type=jnp.float32)  27.6 us
  transfers between devices with their start and end apart: 14, of which 11 were waited for; matrix products, arithmetic and copies ran while one was open for 8% of the time, Pallas kernels for 0%

profile of v1, /device:TPU:0, one launch (start us, length us, event | category | flops | bytes accessed | tf_op | source)
XLA Modules:
  0.0 813.0 jit_solution(3541287029718343683)
XLA Ops:
  10.5 161.8 %collective-permute-done = bf16[1024,2048]{1,0:T(8,128)(2,1)} collective-permute-done((bf16[1024,2048]{1,0:T(8,128)(2,1)}, bf16[1024,2048]{1,0:T(8,128)(2,1)}, u32[]{:S(2)}, u32[]{:S(2)}) %collective-permute-start) | collective-permute-done | bytes 4194336 | tf_op jit(solution)/shard_map/ppermute | solution.py:21
  172.2 6.9 collective-permute-start.2
  180.5 6.7 broadcast_in_dim.117
  198.9 37.7 %collective-permute-done.2 = bf16[1024,2048]{1,0:T(8,128)(2,1)} collective-permute-done((bf16[1024,2048]{1,0:T(8,128)(2,1)}, bf16[1024,2048]{1,0:T(8,128)(2,1)}, u32[]{:S(2)}, u32[]{:S(2)}) %collective-permute-start.2) | collective-permute-done | bytes 4194336 | tf_op jit(solution)/shard_map/ppermute | solution.py:21
  241.5 8.9 %bitcast_dynamic-update-slice_fusion.1 = (bf16[2,64,2048]{2,1,0:T(8,128)(2,1)S(1)}, f32[64,2048]{1,0:T(8,128)S(1)}) fusion(bf16[2,64,2048]{2,1,0:T(8,128)(2,1)S(1)} %broadcast_in_dim.116, s32[]{:T(128)S(6)} %min.19, pred[]{:T(512)S(6)} %and.75, bf16[1,4096,2048]{2,1,0:T(8,128)(2,1)} %all-gather.3.cloned.1.call-done, f32[4096]{0:T(1024)S(1)} %bitcast.221, ...), kind=kOutput, calls=%fused_computation.228 | convolution fusion | flops 1075838976 | bytes 18104838 | tf_op jit(solution)/shard_map/dot_general | solution.py:66
  250.4 11.9 %convolution_convert_fusion.4 = bf16[64,4096]{1,0:T(8,128)(2,1)} fusion(bf16[4096,2048]{1,0:T(8,128)(2,1)} %constant_dynamic-update-slice_fusion.2, f32[64,2048]{1,0:T(8,128)S(1)} %get-tuple-element.165), kind=kOutput, calls=%fused_computation.121 | convolution fusion | flops 1074659328 | bytes 17825792 | tf_op jit(solution)/shard_map/dot_general | solution.py:68
  262.5 40.7 %all-reduce.5.cloned.1.call-done = bf16[64,4096]{1,0:T(8,128)(2,1)} async-done(((bf16[64,4096]{1,0:T(8,128)(2,1)}), bf16[64,4096]{1,0:T(8,128)(2,1)}) %all-reduce.5.cloned.1.call-update) | async-done | bytes 524304 | tf_op jit(solution)/shard_map/psum | solution.py:71
  308.2 9.8 %collective-permute-done.3 = bf16[64,4096]{1,0:T(8,128)(2,1)S(1)} collective-permute-done((bf16[64,4096]{1,0:T(8,128)(2,1)S(1)}, bf16[64,4096]{1,0:T(8,128)(2,1)S(1)}, u32[]{:S(2)}, u32[]{:S(2)}) %collective-permute-start.3) | collective-permute-done | bytes 524320 | tf_op jit(solution)/shard_map/ppermute | solution.py:34
  318.4 9.7 %fusion.170 = (bf16[2,64,2048]{2,1,0:T(8,128)(2,1)S(1)}, f32[64,2048]{1,0:T(8,128)}) fusion(bf16[2,64,2048]{2,1,0:T(8,128)(2,1)S(1)} %get-tuple-element.164, s32[]{:T(128)S(6)} %min.20, pred[]{:T(512)S(6)} %and.76, bf16[1,4096,2048]{2,1,0:T(8,128)(2,1)} %all-gather.3.cloned.1.call-done, bf16[64,4096]{1,0:T(8,128)(2,1)S(1)} %get-tuple-element.148, ...), kind=kOutput, calls=%fused_computation.227 | convolution fusion | flops 1075576832 | bytes 18366980 | tf_op jit(solution)/shard_map/dot_general | solution.py:66
  328.1 12.1 %convolution_convert_fusion.3 = bf16[64,4096]{1,0:T(8,128)(2,1)} fusion(bf16[4096,2048]{1,0:T(8,128)(2,1)} %constant_dynamic-update-slice_fusion.2, f32[64,2048]{1,0:T(8,128)} %get-tuple-element.167), kind=kOutput, calls=%fused_computation.120 | convolution fusion | flops 1074659328 | bytes 17825792 | tf_op jit(solution)/shard_map/dot_general | solution.py:68
  343.1 36.6 %all-reduce.7.cloned.1.call-done = bf16[64,4096]{1,0:T(8,128)(2,1)} async-done(((bf16[64,4096]{1,0:T(8,128)(2,1)}), bf16[64,4096]{1,0:T(8,128)(2,1)}) %all-reduce.7.cloned.1.call-update) | async-done | bytes 524304 | tf_op jit(solution)/shard_map/psum | solution.py:71
  389.6 5.0 collective-permute-done.4
  395.0 9.0 %fusion.169 = (bf16[2,64,2048]{2,1,0:T(8,128)(2,1)S(1)}, f32[64,2048]{1,0:T(8,128)S(1)}) fusion(bf16[2,64,2048]{2,1,0:T(8,128)(2,1)S(1)} %copy-done.4, s32[]{:T(128)S(6)} %min.21, pred[]{:T(512)S(6)} %and.80, bf16[1,4096,2048]{2,1,0:T(8,128)(2,1)} %all-gather.3.cloned.1.call-done, bf16[64,4096]{1,0:T(8,128)(2,1)S(1)} %get-tuple-element.146, ...), kind=kOutput, calls=%fused_computation.225 | convolution fusion | flops 1075576832 | bytes 18366980 | tf_op jit(solution)/shard_map/dot_general | solution.py:66
  406.7 15.7 %fusion.94 = bf16[64,4096]{1,0:T(8,128)(2,1)} fusion(bf16[1,4096,2048]{2,1,0:T(8,128)(2,1)} %all-gather.3.cloned.1.call-done, bf16[4096,2048]{1,0:T(8,128)(2,1)} %constant_dynamic-update-slice_fusion.2, f32[2,64,2048]{2,1,0:T(8,128)} %fusion.152, s32[]{:T(128)S(6)} %min.22, bf16[2,64,4096]{2,1,0:T(8,128)(2,1)S(1)} %copy-done.2, pred[]{:T(512)S(6)} %eq.63), kind=kOutput, calls=%fused_computation.122 | convolution fusion | flops 2149187584 | bytes 35127300 | tf_op jit(solution)/shard_map/dot_general | solution.py:79
  424.5 37.3 %all-reduce.9.cloned.1.call-done = bf16[64,4096]{1,0:T(8,128)(2,1)} async-done(((bf16[64,4096]{1,0:T(8,128)(2,1)}), bf16[64,4096]{1,0:T(8,128)(2,1)}) %all-reduce.9.cloned.1.call-update) | async-done | bytes 524304 | tf_op jit(solution)/shard_map/psum | solution.py:82
  467.3 12.2 %collective-permute-done.5 = bf16[64,4096]{1,0:T(8,128)(2,1)} collective-permute-done((bf16[64,4096]{1,0:T(8,128)(2,1)S(1)}, bf16[64,4096]{1,0:T(8,128)(2,1)}, u32[]{:S(2)}, u32[]{:S(2)}) %collective-permute-start.5) | collective-permute-done | bytes 524320 | tf_op jit(solution)/shard_map/ppermute | solution.py:34
  481.8 15.8 %fusion.97 = bf16[64,4096]{1,0:T(8,128)(2,1)} fusion(bf16[1,4096,2048]{2,1,0:T(8,128)(2,1)} %all-gather.3.cloned.1.call-done, bf16[64,4096]{1,0:T(8,128)(2,1)S(1)} %get-tuple-element.144, bf16[4096,2048]{1,0:T(8,128)(2,1)} %constant_dynamic-update-slice_fusion.2, f32[2,64,2048]{2,1,0:T(8,128)} %fusion.152, s32[]{:T(128)S(6)} %min.23), kind=kOutput, calls=%fused_computation.123 | convolution fusion | flops 2148925440 | bytes 35127300 | tf_op jit(solution)/shard_map/dot_general | solution.py:79
  507.4 4.8 all-to-all-start
  512.2 22.8 %all-reduce.11.cloned.1.call-done = bf16[64,4096]{1,0:T(8,128)(2,1)} async-done(((bf16[64,4096]{1,0:T(8,128)(2,1)}), bf16[64,4096]{1,0:T(8,128)(2,1)}) %all-reduce.11.cloned.1.call-update) | async-done | bytes 524304 | tf_op jit(solution)/shard_map/psum | solution.py:82
  539.1 13.3 %collective-permute-done.6 = bf16[64,4096]{1,0:T(8,128)(2,1)S(1)} collective-permute-done((bf16[64,4096]{1,0:T(8,128)(2,1)S(1)}, bf16[64,4096]{1,0:T(8,128)(2,1)S(1)}, u32[]{:S(2)}, u32[]{:S(2)}) %collective-permute-start.6) | collective-permute-done | bytes 524320 | tf_op jit(solution)/shard_map/ppermute | solution.py:34
  563.9 5.0 all-to-all-start.1
  569.0 6.4 copy.34
  575.4 41.7 %all-to-all-done.1 = bf16[128,32,512]{2,0,1:T(8,128)(2,1)} async-done(((bf16[128,32,512]{2,0,1:T(8,128)(2,1)}), bf16[128,32,512]{2,0,1:T(8,128)(2,1)}, u32[]{:S(2)}, u32[]{:S(2)}) %all-to-all-start.1) | async-done | bytes 4194336 | tf_op jit(solution)/shard_map/all_to_all | solution.py:170
  617.1 10.9 %convolution_convert_fusion.2 = bf16[4,8,512,512]{3,2,1,0:T(8,128)(2,1)} fusion(bf16[4,128,8,512]{1,3,2,0:T(8,128)(2,1)} %bitcast.217, bf16[4,128,8,512]{3,1,2,0:T(8,128)(2,1)} %bitcast.37), kind=kOutput, calls=%fused_computation.112 | convolution fusion | flops 2155872256 | bytes 25165824 | tf_op jit(solution)/shard_map/snbk,snbl->sbkl/dot_general | solution.py:174
  628.0 9.6 %convert_reduce_fusion = f32[8,512,512]{2,1,0:T(8,128)S(1)} fusion(bf16[4,8,512,512]{3,2,1,0:T(8,128)(2,1)} %convolution_convert_fusion.2), kind=kLoop, calls=%fused_computation.101 | loop fusion | flops 14680064 | bytes 25165824 | tf_op jit(solution)/shard_map/reduce_sum | solution.py:176
  637.6 19.7 %bitcast_add_fusion = f32[8,512,512]{2,1,0:T(8,128)} fusion(f32[1,8,512,512]{3,2,1,0:T(8,128)} %param.22, f32[8,512,512]{2,1,0:T(8,128)S(1)} %convert_reduce_fusion), kind=kOutput, calls=%fused_computation.113 | convolution fusion | flops 12893290496 | bytes 25165824 | tf_op jit(solution)/shard_map/sji,sjk->sik/dot_general | solution.py:184
  657.3 17.6 %bitcast_add_fusion.1 = f32[8,512,512]{2,1,0:T(8,128)} fusion(f32[1,8,512,512]{3,2,1,0:T(8,128)} %param.21, f32[8,512,512]{2,1,0:T(8,128)S(1)} %convert_reduce_fusion), kind=kOutput, calls=%fused_computation.114 | convolution fusion | flops 12893290496 | bytes 25165824 | tf_op jit(solution)/shard_map/sij,skj->sik/dot_general | solution.py:180
  674.9 118.8 %while.12 = (s32[]{:T(128)}, bf16[8,512,512]{2,1,0:T(8,128)(2,1)}, bf16[8,512,512]{2,1,0:T(8,128)(2,1)}, pred[8]{0:T(512)(128)(4,1)S(1)}, bf16[8,512,512]{2,1,0:...) while((s32[]{:T(128)}, bf16[8,512,512]{2,1,0:T(8,128)(2,1)}, ...), condition=%wide.region_18.19_spmd, body=%wide.region_13.18_spmd.sunk | while | flops 16121331712 | bytes 28315412 | solution.py:205
  687.1 31.3 %conditional.2 = (bf16[1,512,512]{2,1,0:T(8,128)(2,1)S(1)}, bf16[1,512,512]{2,1,0:T(8,128)(2,1)S(1)}) conditional(s32[]{:T(128)} %bitcast.211, (bf16[8,512,512]{2,1,0:T(8,128)(2,1)}, s32[]{:T(128)}, bf16[8,512,512]{2,1,0:T(8,128)(2,1)}) %tuple.65, (f32[8,512,512]{2,1,0:T(8,128)}, s32[]{:T(128)}, f32[8,512,512]{2,1,0:T(8,128)}) %tuple.66), branch_computations={%region_14.14_spmd, %region_15.17_spmd} | conditional | flops 16121331712 | bytes 26217596 | solution.py:195
  720.6 31.2 %conditional.2 = (bf16[1,512,512]{2,1,0:T(8,128)(2,1)S(1)}, bf16[1,512,512]{2,1,0:T(8,128)(2,1)S(1)}) conditional(s32[]{:T(128)} %bitcast.211, (bf16[8,512,512]{2,1,0:T(8,128)(2,1)}, s32[]{:T(128)}, bf16[8,512,512]{2,1,0:T(8,128)(2,1)}) %tuple.65, (f32[8,512,512]{2,1,0:T(8,128)}, s32[]{:T(128)}, f32[8,512,512]{2,1,0:T(8,128)}) %tuple.66), branch_computations={%region_14.14_spmd, %region_15.17_spmd} | conditional | flops 16121331712 | bytes 26217596 | solution.py:195
  754.1 31.2 %conditional.2 = (bf16[1,512,512]{2,1,0:T(8,128)(2,1)S(1)}, bf16[1,512,512]{2,1,0:T(8,128)(2,1)S(1)}) conditional(s32[]{:T(128)} %bitcast.211, (bf16[8,512,512]{2,1,0:T(8,128)(2,1)}, s32[]{:T(128)}, bf16[8,512,512]{2,1,0:T(8,128)(2,1)}) %tuple.65, (f32[8,512,512]{2,1,0:T(8,128)}, s32[]{:T(128)}, f32[8,512,512]{2,1,0:T(8,128)}) %tuple.66), branch_computations={%region_14.14_spmd, %region_15.17_spmd} | conditional | flops 16121331712 | bytes 26217596 | solution.py:195
  793.7 12.3 %convert_bitcast_fusion = bf16[1,8,512,512]{3,2,1,0:T(8,128)(2,1)} fusion(bf16[8,512,512]{2,1,0:T(8,128)(2,1)} %get-tuple-element.120, bf16[8,512,512]{2,1,0:T(8,128)(2,1)} %get-tuple-element.121, f32[8,512,512]{2,1,0:T(8,128)} %copy-done), kind=kOutput, calls=%fused_computation.127 | convolution fusion | flops 4303355904 | bytes 20971520 | tf_op jit(solution)/shard_map/sij,sjk->sik/dot_general | solution.py:212
  (158 shorter events, 191.7 us)
Async XLA Ops:
  7.2 234.3 %all-gather.3.cloned.1.call-start = ((), (), s32[]{:S(2)}) async-start(), calls=%async_computation.6 | async-start | bytes 20971520 | tf_op jit(solution)/shard_map/all_gather | solution.py:116
  7.9 295.2 %all-reduce.5.cloned.1.call-start = ((), (), s32[]{:S(2)}) async-start(), calls=%async_computation.2 | async-start | bytes 1048576 | tf_op jit(solution)/shard_map/psum | solution.py:71
  7.9 164.3 %collective-permute-start = (bf16[1024,2048]{1,0:T(8,128)(2,1)}, bf16[1024,2048]{1,0:T(8,128)(2,1)}, u32[]{:S(2)}, u32[]{:S(2)}) collective-permute-start(bf16[1024,2048]{1,0:T(8,128)(2,1)} %bitcast.218), channel_id=1, source_target_pairs={{0,4},{4,8},{8,12},{12,0},{1,5},{5,9},{9,13},{13,1},{2,6},{6,10},{... | collective-permute-start | bytes 12582920 | tf_op jit(solution)/shard_map/ppermute | solution.py:21
  8.5 185.6 %collective-permute-start.1 = (bf16[1024,2048]{1,0:T(8,128)(2,1)}, bf16[1024,2048]{1,0:T(8,128)(2,1)}, u32[]{:S(2)}, u32[]{:S(2)}) collective-permute-start(bf16[1024,2048]{1,0:T(8,128)(2,1)} %bitcast.219), channel_id=1, source_target_pairs={{0,12},{4,0},{8,4},{12,8},{1,13},{5,1},{9,5},{13,9},{2,14},{6,2},{... | collective-permute-start | bytes 12582920 | tf_op jit(solution)/shard_map/ppermute | solution.py:24
  172.2 64.5 %collective-permute-start.2 = (bf16[1024,2048]{1,0:T(8,128)(2,1)}, bf16[1024,2048]{1,0:T(8,128)(2,1)}, u32[]{:S(2)}, u32[]{:S(2)}) collective-permute-start(bf16[1024,2048]{1,0:T(8,128)(2,1)} %collective-permute-done), channel_id=1, source_target_pairs={{0,4},{4,8},{8,12},{12,0},{1,5},{5,9},{9,13},{13,1},{2,6},{6,10},{... | collective-permute-start | bytes 12582920 | tf_op jit(solution)/shard_map/ppermute | solution.py:21
  180.5 6.7 copy-start.8
  194.1 47.4 %copy-start.1 = (bf16[2,64,4096]{2,1,0:T(8,128)(2,1)S(1)}, bf16[2,64,4096]{2,1,0:T(8,128)(2,1)}, u32[]{:S(2)}) copy-start(bf16[2,64,4096]{2,1,0:T(8,128)(2,1)} %param.16) | copy-start | bytes 3145732
  194.1 47.4 %copy-start.9 = (f32[1,4096]{1,0:T(1,128)S(1)}, f32[1,4096]{1,0:T(1,128)}, u32[]{:S(2)}) copy-start(f32[1,4096]{1,0:T(1,128)} %param.18) | copy-start | bytes 49156
  250.4 12.0 %copy-start.7 = (f32[64,2048]{1,0:T(8,128)}, f32[64,2048]{1,0:T(8,128)S(1)}, u32[]{:S(2)}) copy-start(f32[64,2048]{1,0:T(8,128)S(1)} %get-tuple-element.165) | copy-start | bytes 1572868
  262.4 117.3 %all-reduce.7.cloned.1.call-start = ((), (), s32[]{:S(2)}) async-start(), calls=%async_computation.3 | async-start | bytes 1048576 | tf_op jit(solution)/shard_map/psum | solution.py:71
  304.3 13.6 %collective-permute-start.3 = (bf16[64,4096]{1,0:T(8,128)(2,1)S(1)}, bf16[64,4096]{1,0:T(8,128)(2,1)S(1)}, u32[]{:S(2)}, u32[]{:S(2)}) collective-permute-start(bf16[64,4096]{1,0:T(8,128)(2,1)S(1)} %fusion.128), channel_id=1, source_target_pairs={{0,16},{1,17},{2,18},{3,19},{4,20},{5,21},{6,22},{7,23},{8,24},{9,... | collective-permute-start | bytes 1572872 | tf_op jit(solution)/shard_map/ppermute | solution.py:34
  328.1 13.2 %copy-start.3 = (bf16[2,64,2048]{2,1,0:T(8,128)(2,1)}, bf16[2,64,2048]{2,1,0:T(8,128)(2,1)S(1)}, u32[]{:S(2)}) copy-start(bf16[2,64,2048]{2,1,0:T(8,128)(2,1)S(1)} %get-tuple-element.166) | copy-start | bytes 1572868
  328.1 12.9 %copy-start.10 = (s32[2,16,8]{1,2,0:T(8,128)S(1)}, s32[2,16,8]{1,2,0:T(8,128)}, u32[]{:S(2)}) copy-start(s32[2,16,8]{1,2,0:T(8,128)} %param.26) | copy-start | bytes 3076
  328.1 12.9 %copy-start.11 = (s32[2,16,8]{1,2,0:T(8,128)S(1)}, s32[2,16,8]{1,2,0:T(8,128)}, u32[]{:S(2)}) copy-start(s32[2,16,8]{1,2,0:T(8,128)} %param.25) | copy-start | bytes 3076
  340.3 121.6 %all-reduce.9.cloned.1.call-start = ((), (), s32[]{:S(2)}) async-start(), calls=%async_computation.4 | async-start | bytes 1048576 | tf_op jit(solution)/shard_map/psum | solution.py:82
  379.7 15.3 %copy-start.4 = (bf16[2,64,2048]{2,1,0:T(8,128)(2,1)S(1)}, bf16[2,64,2048]{2,1,0:T(8,128)(2,1)}, u32[]{:S(2)}) copy-start(bf16[2,64,2048]{2,1,0:T(8,128)(2,1)} %copy-done.3) | copy-start | bytes 1572868
  380.9 13.6 %collective-permute-start.4 = (bf16[64,4096]{1,0:T(8,128)(2,1)S(1)}, bf16[64,4096]{1,0:T(8,128)(2,1)S(1)}, u32[]{:S(2)}, u32[]{:S(2)}) collective-permute-start(bf16[64,4096]{1,0:T(8,128)(2,1)S(1)} %fusion.120), channel_id=1, source_target_pairs={{0,16},{1,17},{2,18},{3,19},{4,20},{5,21},{6,22},{7,23},{8,24},{9,... | collective-permute-start | bytes 1572872 | tf_op jit(solution)/shard_map/ppermute | solution.py:34
  395.0 11.7 %copy-start.2 = (bf16[2,64,4096]{2,1,0:T(8,128)(2,1)S(1)}, bf16[2,64,4096]{2,1,0:T(8,128)(2,1)}, u32[]{:S(2)}) copy-start(bf16[2,64,4096]{2,1,0:T(8,128)(2,1)} %param.17) | copy-start | bytes 3145732
  404.0 0.8 copy-start.5
  422.5 112.6 %all-reduce.11.cloned.1.call-start = ((), (), s32[]{:S(2)}) async-start(), calls=%async_computation.5 | async-start | bytes 1048576 | tf_op jit(solution)/shard_map/psum | solution.py:82
  464.8 14.7 %collective-permute-start.5 = (bf16[64,4096]{1,0:T(8,128)(2,1)S(1)}, bf16[64,4096]{1,0:T(8,128)(2,1)}, u32[]{:S(2)}, u32[]{:S(2)}) collective-permute-start(bf16[64,4096]{1,0:T(8,128)(2,1)S(1)} %fusion.122), channel_id=1, source_target_pairs={{16,0},{17,1},{18,2},{19,3},{20,4},{21,5},{22,6},{23,7},{24,8},{25... | collective-permute-start | bytes 1572872 | tf_op jit(solution)/shard_map/ppermute | solution.py:34
  481.8 15.8 %copy-start.6 = (bf16[2,64,2048]{2,1,0:T(8,128)(2,1)S(1)}, bf16[2,64,2048]{2,1,0:T(8,128)(2,1)}, u32[]{:S(2)}) copy-start(bf16[2,64,2048]{2,1,0:T(8,128)(2,1)} %copy-done.5) | copy-start | bytes 1572868
  507.4 56.5 %all-to-all-start = ((bf16[128,32,512]{2,0,1:T(8,128)(2,1)}), bf16[128,32,512]{2,0,1:T(8,128)(2,1)}, u32[]{:S(2)}, u32[]{:S(2)}) async-start(bf16[128,32,512]{2,0,1:T(8,128)(2,1)} %select_bitcast_fusion.1), calls=%async_computation | async-start | bytes 8388608 | tf_op jit(solution)/shard_map/all_to_all | solution.py:169
  537.8 14.6 %collective-permute-start.6 = (bf16[64,4096]{1,0:T(8,128)(2,1)S(1)}, bf16[64,4096]{1,0:T(8,128)(2,1)S(1)}, u32[]{:S(2)}, u32[]{:S(2)}) collective-permute-start(bf16[64,4096]{1,0:T(8,128)(2,1)S(1)} %fusion.124), channel_id=1, source_target_pairs={{16,0},{17,1},{18,2},{19,3},{20,4},{21,5},{22,6},{23,7},{24,8},{25... | collective-permute-start | bytes 1572872 | tf_op jit(solution)/shard_map/ppermute | solution.py:34
  563.9 53.2 %all-to-all-start.1 = ((bf16[128,32,512]{2,0,1:T(8,128)(2,1)}), bf16[128,32,512]{2,0,1:T(8,128)(2,1)}, u32[]{:S(2)}, u32[]{:S(2)}) async-start(bf16[128,32,512]{2,0,1:T(8,128)(2,1)} %select_bitcast_fusion), calls=%async_computation.1 | async-start | bytes 8388608 | tf_op jit(solution)/shard_map/all_to_all | solution.py:170
  637.6 19.7 %copy-start = (f32[8,512,512]{2,1,0:T(8,128)}, f32[8,512,512]{2,1,0:T(8,128)S(1)}, u32[]{:S(2)}) copy-start(f32[8,512,512]{2,1,0:T(8,128)S(1)} %convert_reduce_fusion) | copy-start | bytes 25165828
Sparse Core Ops, SparseCore 0:
  9.5 191.5 all-gather.2
  262.5 40.5 all-reduce.4
  340.4 39.2 all-reduce.6
  422.6 39.1 all-reduce.8
  497.7 37.3 all-reduce.10
